TPU v7x, 512 devices: a whole 4x4x16 slice. The times are simulated.
512 devices in a mesh: ctx: 64 (over y, z), ch: 8 (over x, core).
Axes of the slice: x: 4, y: 4, z: 16, core: 2. Of those that a mesh axis runs over, the one named last changes fastest.
Arguments:
- query_input: bfloat16 [8192, 1024], P('ctx', 'ch'), may hold values from -6 to 6
- key_input: bfloat16 [8192, 1024], P('ctx', 'ch'), may hold values from -6 to 6
- value_input: bfloat16 [8192, 1024], P('ctx', 'ch'), may hold values from -6 to 6
- implicit_filter: float32 [8192, 1024], P('ctx', 'ch'), may hold values from -1.1 to 1.1
- explicit_taps: float32 [128, 1024], P(None, 'ch'), may hold values from -0.5 to 0.5
- skip_gain: float32 [1024], P('ch'), may hold values from -3 to 3
- out_grad: bfloat16 [8192, 1024], P('ctx', 'ch'), may hold values from -6 to 6
Outputs:
- mixed_output: float32 [8192, 1024], P('ctx', 'ch')
- query_grad: float32 [8192, 1024], P('ctx', 'ch')
- key_grad: float32 [8192, 1024], P('ctx', 'ch')
- value_grad: float32 [8192, 1024], P('ctx', 'ch')
- filter_grad: float32 [8192, 1024], P('ctx', 'ch')
- taps_grad: float32 [128, 1024], P(None, 'ch')
- skip_grad: float32 [1024], P('ch')
All inputs are finite; a program needn't handle non-finite values.
Results may differ from a plain program's by a relative error of at most 0.0005.
Values sent between devices are 32-bit elements; how exact they have to be, the bound alone decides.
A program may use at most 64 MiB of HBM per device.

v0:
```python
import math

import jax
import jax.numpy as jnp
from jax import lax
from jax.sharding import PartitionSpec as P


def from_partner(value, axis, stride):
    mask = 2**stride
    pairs = [(source, source ^ mask) for source in range(lax.axis_size(axis))]
    return lax.ppermute(value, axis, pairs)


def from_behind(value, axis, by):
    length = lax.axis_size(axis)
    pairs = [(i, i + by) for i in range(length) if 0 <= i + by < length]
    return lax.ppermute(value, axis, pairs)


def reversed_bits(values, section_count):
    flipped = jnp.zeros_like(values)
    for section_level in range(section_count):
        flipped = flipped + values // 2**section_level % 2 * 2 ** (
            section_count - 1 - section_level
        )
    return flipped


def rotate_parts(real_part, imag_part, phase_angle):
    cosine = jnp.cos(phase_angle)
    sine_value = jnp.sin(phase_angle)
    return (
        real_part * cosine - imag_part * sine_value,
        real_part * sine_value + imag_part * cosine,
    )


def rotate_spectra(spectra, phase_angle):
    real_part, imag_part = rotate_parts(spectra[:, :, 0], spectra[:, :, 1], phase_angle)
    return jnp.stack([real_part, imag_part], axis=2)


def half_shift(real_fields, shard_pos, shard_count):
    phase_angle = -math.pi * shard_pos.astype(jnp.float32) / shard_count
    empty_part = jnp.zeros_like(real_fields)
    plain_pair = jnp.stack([real_fields, empty_part], axis=1)
    turned_pair = jnp.stack(
        [real_fields * jnp.cos(phase_angle), real_fields * jnp.sin(phase_angle)], axis=1
    )
    return jnp.stack([plain_pair, turned_pair], axis=1)


def butterfly_down(own_data, partner_data, upper_half, offset, half_span):
    phase_angle = -math.pi * offset.astype(jnp.float32) / half_span
    summed = own_data + partner_data
    turned = rotate_spectra(partner_data - own_data, phase_angle)
    return jnp.where(upper_half == 1, turned, summed)


def butterfly_up(own_data, partner_data, upper_half, offset, half_span):
    phase_angle = math.pi * offset.astype(jnp.float32) / half_span
    summed = own_data + rotate_spectra(partner_data, phase_angle)
    turned = partner_data - rotate_spectra(own_data, phase_angle)
    return jnp.where(upper_half == 1, turned, summed)


def pair_forward(real_fields, shard_count, shard_index):
    section_count = shard_count.bit_length() - 1
    top_level = section_count - 1
    half_span = 2**top_level
    upper_half = shard_index // half_span % 2
    partner_index = shard_index + half_span - 2 * half_span * upper_half
    partner_real = from_partner(real_fields, "ctx", top_level)
    spectra = butterfly_down(
        half_shift(real_fields, shard_index, shard_count),
        half_shift(partner_real, partner_index, shard_count),
        upper_half,
        shard_index % half_span,
        half_span,
    )
    for section_level in range(top_level - 1, -1, -1):
        half_span = 2**section_level
        upper_half = shard_index // half_span % 2
        partner_data = from_partner(spectra, "ctx", section_level)
        spectra = butterfly_down(
            spectra, partner_data, upper_half, shard_index % half_span, half_span
        )
    return spectra


def pair_inverse(spectra, shard_count, shard_index, extent):
    section_count = shard_count.bit_length() - 1
    top_level = section_count - 1
    for section_level in range(top_level):
        half_span = 2**section_level
        upper_half = shard_index // half_span % 2
        partner_data = from_partner(spectra, "ctx", section_level)
        spectra = butterfly_up(
            spectra, partner_data, upper_half, shard_index % half_span, half_span
        )
    half_span = 2**top_level
    upper_half = shard_index // half_span % 2
    partner_index = shard_index + half_span - 2 * half_span * upper_half
    twist_angle = math.pi * (shard_index % half_span).astype(jnp.float32) / half_span

    def folded(target_index):
        shift_angle = math.pi * target_index.astype(jnp.float32) / shard_count
        sum_real, sum_imag = rotate_parts(spectra[:, 1, 0], spectra[:, 1, 1], shift_angle)
        sum_real = sum_real + spectra[:, 0, 0]
        sum_imag = sum_imag + spectra[:, 0, 1]
        twisted_real, twisted_imag = rotate_parts(sum_real, sum_imag, twist_angle)
        return jnp.where(upper_half == 1, twisted_real, sum_real)

    sent_part = folded(partner_index)
    kept_part = folded(shard_index)
    received = from_partner(sent_part, "ctx", top_level)
    sign_value = (1 - 2 * upper_half).astype(jnp.float32)
    return (sign_value * kept_part + received) / extent


def local_tables(shard_count, shard_index, local_rows):
    section_count = shard_count.bit_length() - 1
    flipped = reversed_bits(shard_index, section_count)
    extent_count = 2 * shard_count * local_rows
    positions = jnp.arange(local_rows, dtype=jnp.int32)
    coarse = (positions[:, None] * positions[None, :] % local_rows).astype(jnp.float32) / local_rows
    first_freq = jnp.stack([2 * flipped, 2 * flipped + 1])
    fine = (positions[None, None, :] * first_freq[:, None, None]).astype(jnp.float32) / extent_count
    phase_angle = -2.0 * math.pi * (coarse[None] + fine)
    cosine = jnp.cos(phase_angle)
    sine_value = jnp.sin(phase_angle)
    forward_table = jnp.stack(
        [jnp.stack([cosine, -sine_value], 1), jnp.stack([sine_value, cosine], 1)], 1
    )
    cosine_turned = jnp.swapaxes(cosine, 1, 2)
    sine_turned = jnp.swapaxes(sine_value, 1, 2)
    inverse_table = jnp.stack(
        [jnp.stack([cosine_turned, sine_turned], 1), jnp.stack([-sine_turned, cosine_turned], 1)], 1
    )
    return (forward_table, inverse_table)


def spectral_products(spectra):
    prod_real, prod_imag = (spectra[0, :, 0], spectra[0, :, 1])
    kern_real, kern_imag = (spectra[1, :, 0], spectra[1, :, 1])
    grad_real, grad_imag = (spectra[2, :, 0], spectra[2, :, 1])
    out_real = kern_real * prod_real - kern_imag * prod_imag
    out_imag = kern_real * prod_imag + kern_imag * prod_real
    back_real = kern_real * grad_real + kern_imag * grad_imag
    back_imag = kern_real * grad_imag - kern_imag * grad_real
    lag_real = prod_real * grad_real + prod_imag * grad_imag
    lag_imag = prod_real * grad_imag - prod_imag * grad_real
    return jnp.stack(
        [
            jnp.stack([out_real, out_imag], 1),
            jnp.stack([back_real, back_imag], 1),
            jnp.stack([lag_real, lag_imag], 1),
        ]
    )


def body(query_input, key_input, value_input, implicit_filter, explicit_taps, skip_gain, out_grad):
    local_rows = query_input.shape[0]
    shard_count = lax.axis_size("ctx")
    shard_index = lax.axis_index("ctx")
    tap_count = explicit_taps.shape[0]
    extent = 2.0 * shard_count * local_rows
    grad_scale = 1.0 / math.sqrt(shard_count * local_rows)
    query_full = query_input.astype(jnp.float32)
    key_full = key_input.astype(jnp.float32)
    value_full = value_input.astype(jnp.float32)
    grad_full = out_grad.astype(jnp.float32)
    product = key_full * value_full
    mix_grad = grad_full * query_full
    earlier = from_behind(product[local_rows - (tap_count - 1) :], "ctx", 1)
    later = from_behind(mix_grad[: tap_count - 1], "ctx", -1)
    before_rows = jnp.concatenate([earlier, product], axis=0)
    after_rows = jnp.concatenate([mix_grad, later], axis=0)
    explicit_part = jnp.zeros_like(product)
    explicit_grad = jnp.zeros_like(product)
    for tap_lag in range(tap_count):
        lagged_rows = before_rows[tap_count - 1 - tap_lag : tap_count - 1 - tap_lag + local_rows]
        explicit_part = explicit_part + explicit_taps[tap_lag] * lagged_rows
        explicit_grad = (
            explicit_grad + explicit_taps[tap_lag] * after_rows[tap_lag : tap_lag + local_rows]
        )
    real_fields = jnp.stack([product, implicit_filter, mix_grad])
    spectra = pair_forward(real_fields, shard_count, shard_index)
    forward_table, inverse_table = local_tables(shard_count, shard_index, local_rows)
    spectra = jnp.einsum(
        "roixy,friyc->froxc", forward_table, spectra, precision=lax.Precision.HIGHEST
    )
    products = spectral_products(spectra)
    products = jnp.einsum(
        "roixy,friyc->froxc", inverse_table, products, precision=lax.Precision.HIGHEST
    )
    results = pair_inverse(products, shard_count, shard_index, extent)
    implicit_part = results[0]
    implicit_grad = results[1]
    lag_grad = results[2]
    tap_local = jnp.where(shard_index == 0, lag_grad, 0.0)
    skip_local = jnp.sum(mix_grad * product, axis=0)
    tap_total, skip_total = lax.psum((tap_local, skip_local), "ctx")
    mixer = implicit_part + explicit_part + skip_gain * product
    mixed_output = query_full * mixer
    query_grad = grad_full * mixer
    product_grad = implicit_grad + explicit_grad + skip_gain * mix_grad
    key_grad = product_grad * value_full
    value_grad = product_grad * key_full
    return (
        mixed_output,
        query_grad,
        key_grad,
        value_grad,
        lag_grad * grad_scale,
        tap_total * grad_scale,
        skip_total * grad_scale,
    )


def solution(mesh):
    in_specs = (
        P("ctx", "ch"),
        P("ctx", "ch"),
        P("ctx", "ch"),
        P("ctx", "ch"),
        P(None, "ch"),
        P("ch"),
        P("ctx", "ch"),
    )
    out_specs = (
        P("ctx", "ch"),
        P("ctx", "ch"),
        P("ctx", "ch"),
        P("ctx", "ch"),
        P("ctx", "ch"),
        P(None, "ch"),
        P("ch"),
    )
    return jax.shard_map(body, mesh=mesh, in_specs=in_specs, out_specs=out_specs, check_vma=False)
```

profile of v0, /device:TPU:1, one launch (start us, length us, event | category | flops | bytes accessed | tf_op | source)
XLA Modules:
  0.0 872.5 jit_solution(15959564310874243135)
XLA Ops:
  7.2 0.9 copy.18
  8.1 0.1 copy.16
  8.2 0.6 copy-done.5
  8.9 0.1 copy.15
  9.0 0.1 copy.14
  9.1 0.6 copy-done.3
  9.8 0.7 multiply_reduce_fusion
  10.5 5.6 collective-permute-start
  16.7 2.5 collective-permute-done
  19.5 1.0 maximum_select_fusion
  20.5 4.5 collective-permute-start.1
  25.2 12.7 %collective-permute-done.1 = f32[3,2,2,128,128]{3,4,2,0,1:T(8,128)S(1)} collective-permute-done((f32[3,2,2,128,128]{3,4,2,0,1:T(8,128)}, f32[3,2,2,128,128]{3,4,2,0,1:T(8,128)S(1)}, u32[]{:S(2)}, u32[]{:S(2)}) %collective-permute-start.1) | collective-permute-done | bytes 786464 | tf_op jit(solution)/shard_map/ppermute | solution.py:12
  37.8 0.2 fusion.819
  38.1 1.1 maximum_select_fusion.1
  39.2 19.0 %collective-permute-start.2 = (f32[3,2,2,128,128]{3,4,2,0,1:T(8,128)}, f32[3,2,2,128,128]{3,4,2,0,1:T(8,128)}, u32[]{:S(2)}, u32[]{:S(2)}) collective-permute-start(f32[3,2,2,128,128]{3,4,2,0,1:T(8,128)} %maximum_select_fusion.1), channel_id=1, source_target_pairs={{0,64},{8,72},{16,80},{24,88},{32,96},{40,104},{48,112},{56,120},{... | collective-permute-start | bytes 2359304 | tf_op jit(solution)/shard_map/ppermute | solution.py:12
  58.5 24.4 %collective-permute-done.2 = f32[3,2,2,128,128]{3,4,2,0,1:T(8,128)} collective-permute-done((f32[3,2,2,128,128]{3,4,2,0,1:T(8,128)}, f32[3,2,2,128,128]{3,4,2,0,1:T(8,128)}, u32[]{:S(2)}, u32[]{:S(2)}) %collective-permute-start.2) | collective-permute-done | bytes 786464 | tf_op jit(solution)/shard_map/ppermute | solution.py:12
  82.9 1.6 fusion.820
  84.6 1.5 maximum_select_fusion.2
  86.1 38.8 %collective-permute-start.3 = (f32[3,2,2,128,128]{3,4,2,0,1:T(8,128)S(1)}, f32[3,2,2,128,128]{3,4,2,0,1:T(8,128)S(1)}, u32[]{:S(2)}, u32[]{:S(2)}) collective-permute-start(f32[3,2,2,128,128]{3,4,2,0,1:T(8,128)S(1)} %maximum_select_fusion.2), channel_id=1, source_target_pairs={{0,32},{8,40},{16,48},{24,56},{32,0},{40,8},{48,16},{56,24},{64,96... | collective-permute-start | bytes 2359304 | tf_op jit(solution)/shard_map/ppermute | solution.py:12
  125.1 70.2 %collective-permute-done.3 = f32[3,2,2,128,128]{3,4,2,0,1:T(8,128)S(1)} collective-permute-done((f32[3,2,2,128,128]{3,4,2,0,1:T(8,128)S(1)}, f32[3,2,2,128,128]{3,4,2,0,1:T(8,128)S(1)}, u32[]{:S(2)}, u32[]{:S(2)}) %collective-permute-start.3) | collective-permute-done | bytes 786464 | tf_op jit(solution)/shard_map/ppermute | solution.py:12
  195.4 0.1 maximum_select_fusion.3
  195.6 1.9 collective-permute-start.4
  197.8 34.3 %collective-permute-done.4 = f32[3,2,2,128,128]{3,4,2,0,1:T(8,128)S(1)} collective-permute-done((f32[3,2,2,128,128]{3,4,2,0,1:T(8,128)S(1)}, f32[3,2,2,128,128]{3,4,2,0,1:T(8,128)S(1)}, u32[]{:S(2)}, u32[]{:S(2)}) %collective-permute-start.4) | collective-permute-done | bytes 786464 | tf_op jit(solution)/shard_map/ppermute | solution.py:12
  232.2 0.1 maximum_select_fusion.4
  232.4 1.9 collective-permute-start.5
  234.4 1.0 fusion.35
  235.5 17.3 %collective-permute-done.5 = f32[3,2,2,128,128]{3,4,2,0,1:T(8,128)S(1)} collective-permute-done((f32[3,2,2,128,128]{3,4,2,0,1:T(8,128)S(1)}, f32[3,2,2,128,128]{3,4,2,0,1:T(8,128)S(1)}, u32[]{:S(2)}, u32[]{:S(2)}) %collective-permute-start.5) | collective-permute-done | bytes 786464 | tf_op jit(solution)/shard_map/ppermute | solution.py:12
  253.0 1.0 convolution_bitcast_fusion.1
  254.2 0.9 convolution_bitcast_fusion
  255.1 2.2 collective-permute-start.6
  257.4 17.4 %collective-permute-done.6 = f32[3,2,2,128,128]{3,4,2,0,1:T(8,128)S(1)} collective-permute-done((f32[3,2,2,128,128]{3,4,2,0,1:T(8,128)S(1)}, f32[3,2,2,128,128]{3,4,2,0,1:T(8,128)S(1)}, u32[]{:S(2)}, u32[]{:S(2)}) %collective-permute-start.6) | collective-permute-done | bytes 786464 | tf_op jit(solution)/shard_map/ppermute | solution.py:12
  274.8 0.2 fusion.4
  275.0 1.9 collective-permute-start.7
  277.2 36.6 %collective-permute-done.7 = f32[3,2,2,128,128]{3,4,2,0,1:T(8,128)S(1)} collective-permute-done((f32[3,2,2,128,128]{3,4,2,0,1:T(8,128)S(1)}, f32[3,2,2,128,128]{3,4,2,0,1:T(8,128)S(1)}, u32[]{:S(2)}, u32[]{:S(2)}) %collective-permute-start.7) | collective-permute-done | bytes 786464 | tf_op jit(solution)/shard_map/ppermute | solution.py:12
  314.0 0.3 fusion.5
  314.3 1.9 collective-permute-start.8
  316.3 2.1 collective-permute-start.12
  318.4 1.3 collective-permute-start.13
  319.9 0.1 multiply_subtract_fusion.5
  320.0 84.1 %collective-permute-done.8 = f32[3,2,2,128,128]{3,4,2,0,1:T(8,128)S(1)} collective-permute-done((f32[3,2,2,128,128]{3,4,2,0,1:T(8,128)S(1)}, f32[3,2,2,128,128]{3,4,2,0,1:T(8,128)S(1)}, u32[]{:S(2)}, u32[]{:S(2)}) %collective-permute-start.8) | collective-permute-done | bytes 786464 | tf_op jit(solution)/shard_map/ppermute | solution.py:12
  404.2 0.3 fusion.6
  404.4 10.0 %collective-permute-start.9 = (f32[3,2,2,128,128]{3,4,2,0,1:T(8,128)S(1)}, f32[3,2,2,128,128]{3,4,2,0,1:T(8,128)S(1)}, u32[]{:S(2)}, u32[]{:S(2)}) collective-permute-start(f32[3,2,2,128,128]{3,4,2,0,1:T(8,128)S(1)} %fusion.6), channel_id=1, source_target_pairs={{0,64},{8,72},{16,80},{24,88},{32,96},{40,104},{48,112},{56,120},{... | collective-permute-start | bytes 2359304 | tf_op jit(solution)/shard_map/ppermute | solution.py:12
  414.8 27.7 %collective-permute-done.9 = f32[3,2,2,128,128]{3,4,2,0,1:T(8,128)S(1)} collective-permute-done((f32[3,2,2,128,128]{3,4,2,0,1:T(8,128)S(1)}, f32[3,2,2,128,128]{3,4,2,0,1:T(8,128)S(1)}, u32[]{:S(2)}, u32[]{:S(2)}) %collective-permute-start.9) | collective-permute-done | bytes 786464 | tf_op jit(solution)/shard_map/ppermute | solution.py:12
  442.7 0.3 fusion.7
  442.9 3.2 collective-permute-start.10
  446.8 130.7 %psum.15 = f32[128]{0:T(128)S(1)} all-reduce(f32[128]{0:T(128)S(1)} %get-tuple-element.72), channel_id=1, replica_groups=mesh['ctx'=64,'ch'=8] {'ctx'}, use_global_device_ids=true, to_apply=%region_2.3 | all-reduce | flops 128 | bytes 1024 | tf_op jit(solution)/shard_map/psum | solution.py:204
  577.7 0.1 multiply_subtract_fusion
  577.8 0.3 fusion.8
  578.1 2.1 collective-permute-start.11
  580.2 0.5 broadcast_multiply_fusion.1
  580.8 5.3 collective-permute-done.11
  586.1 0.1 fusion.20
  586.2 0.6 select_bitcast_fusion
  586.9 0.7 copy-done.7
  587.5 7.1 convert_multiply_fusion
  594.7 7.3 convert_multiply_fusion.4
  602.0 0.7 copy.42
  602.8 0.7 copy.43
  603.5 0.7 copy.44
  604.2 0.7 copy.45
  605.0 0.7 copy.46
  605.7 258.3 %all-reduce.4.cloned.1.call-done = f32[128,128]{0,1:T(8,128)} async-done(((f32[128,128]{0,1:T(8,128)}), f32[128,128]{0,1:T(8,128)}) %all-reduce.4.cloned.1.call-update) | async-done | bytes 65552 | tf_op jit(solution)/shard_map/psum | solution.py:204
  864.0 0.8 broadcast_multiply_fusion
  864.9 0.7 copy.47
  (64 shorter events, 2.6 us)
Async XLA Ops:
  7.2 0.9 copy-start.4
  7.2 856.9 %all-reduce.4.cloned.1.call-start = ((), (), s32[]{:S(2)}) async-start(), calls=%async_computation | async-start | bytes 131072 | tf_op jit(solution)/shard_map/psum | solution.py:204
  8.1 0.8 copy-start.5
  8.1 0.9 copy-start.6
  8.9 0.8 copy-start.3
  10.5 8.7 collective-permute-start
  20.5 17.4 %collective-permute-start.1 = (f32[3,2,2,128,128]{3,4,2,0,1:T(8,128)}, f32[3,2,2,128,128]{3,4,2,0,1:T(8,128)S(1)}, u32[]{:S(2)}, u32[]{:S(2)}) collective-permute-start(f32[3,2,2,128,128]{3,4,2,0,1:T(8,128)} %maximum_select_fusion), channel_id=1, source_target_pairs={{0,128},{8,136},{16,144},{24,152},{32,160},{40,168},{48,176},{56,1... | collective-permute-start | bytes 2359304 | tf_op jit(solution)/shard_map/ppermute | solution.py:12
  38.1 1.2 copy-start
  39.2 43.7 %collective-permute-start.2 = (f32[3,2,2,128,128]{3,4,2,0,1:T(8,128)}, f32[3,2,2,128,128]{3,4,2,0,1:T(8,128)}, u32[]{:S(2)}, u32[]{:S(2)}) collective-permute-start(f32[3,2,2,128,128]{3,4,2,0,1:T(8,128)} %maximum_select_fusion.1), channel_id=1, source_target_pairs={{0,64},{8,72},{16,80},{24,88},{32,96},{40,104},{48,112},{56,120},{... | collective-permute-start | bytes 2359304 | tf_op jit(solution)/shard_map/ppermute | solution.py:12
  86.1 109.2 %collective-permute-start.3 = (f32[3,2,2,128,128]{3,4,2,0,1:T(8,128)S(1)}, f32[3,2,2,128,128]{3,4,2,0,1:T(8,128)S(1)}, u32[]{:S(2)}, u32[]{:S(2)}) collective-permute-start(f32[3,2,2,128,128]{3,4,2,0,1:T(8,128)S(1)} %maximum_select_fusion.2), channel_id=1, source_target_pairs={{0,32},{8,40},{16,48},{24,56},{32,0},{40,8},{48,16},{56,24},{64,96... | collective-permute-start | bytes 2359304 | tf_op jit(solution)/shard_map/ppermute | solution.py:12
  195.6 36.5 %collective-permute-start.4 = (f32[3,2,2,128,128]{3,4,2,0,1:T(8,128)S(1)}, f32[3,2,2,128,128]{3,4,2,0,1:T(8,128)S(1)}, u32[]{:S(2)}, u32[]{:S(2)}) collective-permute-start(f32[3,2,2,128,128]{3,4,2,0,1:T(8,128)S(1)} %maximum_select_fusion.3), channel_id=1, source_target_pairs={{0,16},{8,24},{16,0},{24,8},{32,48},{40,56},{48,32},{56,40},{64,80... | collective-permute-start | bytes 2359304 | tf_op jit(solution)/shard_map/ppermute | solution.py:12
  232.4 20.5 %collective-permute-start.5 = (f32[3,2,2,128,128]{3,4,2,0,1:T(8,128)S(1)}, f32[3,2,2,128,128]{3,4,2,0,1:T(8,128)S(1)}, u32[]{:S(2)}, u32[]{:S(2)}) collective-permute-start(f32[3,2,2,128,128]{3,4,2,0,1:T(8,128)S(1)} %maximum_select_fusion.4), channel_id=1, source_target_pairs={{0,8},{8,0},{16,24},{24,16},{32,40},{40,32},{48,56},{56,48},{64,72... | collective-permute-start | bytes 2359304 | tf_op jit(solution)/shard_map/ppermute | solution.py:12
  255.1 19.7 %collective-permute-start.6 = (f32[3,2,2,128,128]{3,4,2,0,1:T(8,128)S(1)}, f32[3,2,2,128,128]{3,4,2,0,1:T(8,128)S(1)}, u32[]{:S(2)}, u32[]{:S(2)}) collective-permute-start(f32[3,2,2,128,128]{3,4,2,0,1:T(8,128)S(1)} %convolution_bitcast_fusion), channel_id=1, source_target_pairs={{0,8},{8,0},{16,24},{24,16},{32,40},{40,32},{48,56},{56,48},{64,72... | collective-permute-start | bytes 2359304 | tf_op jit(solution)/shard_map/ppermute | solution.py:12
  275.0 38.8 %collective-permute-start.7 = (f32[3,2,2,128,128]{3,4,2,0,1:T(8,128)S(1)}, f32[3,2,2,128,128]{3,4,2,0,1:T(8,128)S(1)}, u32[]{:S(2)}, u32[]{:S(2)}) collective-permute-start(f32[3,2,2,128,128]{3,4,2,0,1:T(8,128)S(1)} %fusion.4), channel_id=1, source_target_pairs={{0,16},{8,24},{16,0},{24,8},{32,48},{40,56},{48,32},{56,40},{64,80... | collective-permute-start | bytes 2359304 | tf_op jit(solution)/shard_map/ppermute | solution.py:12
  314.3 89.8 %collective-permute-start.8 = (f32[3,2,2,128,128]{3,4,2,0,1:T(8,128)S(1)}, f32[3,2,2,128,128]{3,4,2,0,1:T(8,128)S(1)}, u32[]{:S(2)}, u32[]{:S(2)}) collective-permute-start(f32[3,2,2,128,128]{3,4,2,0,1:T(8,128)S(1)} %fusion.5), channel_id=1, source_target_pairs={{0,32},{8,40},{16,48},{24,56},{32,0},{40,8},{48,16},{56,24},{64,96... | collective-permute-start | bytes 2359304 | tf_op jit(solution)/shard_map/ppermute | solution.py:12
  316.2 2.2 copy-start.1
  316.2 3.7 copy-start.2
  316.3 270.6 %collective-permute-start.12 = (f32[127,128]{0,1:T(8,128)S(1)}, f32[127,128]{0,1:T(8,128)S(1)}, u32[]{:S(2)}, u32[]{:S(2)}) collective-permute-start(f32[127,128]{0,1:T(8,128)S(1)} %slice.1891), channel_id=1, source_target_pairs={{0,8},{8,16},{16,24},{24,32},{32,40},{40,48},{48,56},{56,64},{64,7... | collective-permute-start | bytes 195080 | tf_op jit(solution)/shard_map/ppermute | solution.py:18
  318.4 276.3 %collective-permute-start.13 = (f32[127,128]{0,1:T(8,128)S(1)}, f32[127,128]{0,1:T(8,128)S(1)}, u32[]{:S(2)}, u32[]{:S(2)}) collective-permute-start(f32[127,128]{0,1:T(8,128)S(1)} %bitcast.507), channel_id=1, source_target_pairs={{8,0},{16,8},{24,16},{32,24},{40,32},{48,40},{56,48},{64,56},{72,6... | collective-permute-start | bytes 195080 | tf_op jit(solution)/shard_map/ppermute | solution.py:18
  404.4 38.1 %collective-permute-start.9 = (f32[3,2,2,128,128]{3,4,2,0,1:T(8,128)S(1)}, f32[3,2,2,128,128]{3,4,2,0,1:T(8,128)S(1)}, u32[]{:S(2)}, u32[]{:S(2)}) collective-permute-start(f32[3,2,2,128,128]{3,4,2,0,1:T(8,128)S(1)} %fusion.6), channel_id=1, source_target_pairs={{0,64},{8,72},{16,80},{24,88},{32,96},{40,104},{48,112},{56,120},{... | collective-permute-start | bytes 2359304 | tf_op jit(solution)/shard_map/ppermute | solution.py:12
  442.9 134.7 %collective-permute-start.10 = (f32[3,2,2,128,128]{3,4,2,0,1:T(8,128)S(1)}, f32[3,2,2,128,128]{3,4,2,0,1:T(8,128)S(1)}, u32[]{:S(2)}, u32[]{:S(2)}) collective-permute-start(f32[3,2,2,128,128]{3,4,2,0,1:T(8,128)S(1)} %fusion.7), channel_id=1, source_target_pairs={{0,128},{8,136},{16,144},{24,152},{32,160},{40,168},{48,176},{56,1... | collective-permute-start | bytes 2359304 | tf_op jit(solution)/shard_map/ppermute | solution.py:12
  578.1 8.0 collective-permute-start.11
  586.9 0.7 copy-start.7
Sparse Core Ops, SparseCore 0:
  594.8 269.2 all-reduce.3
where the time goes:
time: 884 us; the launch traced here: 872 us
  waiting for transfers between devices  591 us (67%)
  blocking collectives  131 us (15%)
  starting transfers between devices  96.6 us (11%)
  other arithmetic  27.6 us (3%)
  between operations  17.1 us (2%)
    ppermute x12, waiting for transfers between devices, from_partner(): return lax.ppermute(value, axis, pairs)  333 us
    psum x1, waiting for transfers between devices, body(): tap_total, skip_total = lax.psum((tap_local, skip_local), 'ctx')  258 us
    psum x1, blocking collectives, body(): tap_total, skip_total = lax.psum((tap_local, skip_local), 'ctx')  131 us
    ppermute x12, starting transfers between devices, from_partner(): return lax.ppermute(value, axis, pairs)  93.2 us
  transfers between devices with their start and end apart: 15, of which 12 were waited for; matrix products, arithmetic and copies ran while one was open for 3% of the time, Pallas kernels for 0%

commit v1 on v0

v1 whole, which is shorter than its diff:
```python
import math

import jax
import jax.numpy as jnp
import numpy as np
from jax import lax
from jax.sharding import PartitionSpec as P


def tables(blocks, rows):
    s = np.arange(blocks)
    t = np.arange(rows)
    k1 = s + 0.25
    outer = 2 * np.pi * np.outer(k1, s) / blocks
    first = np.concatenate([np.cos(outer), -np.sin(outer)], axis=0)
    turn = 2 * np.pi * np.outer(k1, t) / (blocks * rows)
    inner = 2 * np.pi * (np.outer(t, t) % rows) / rows
    c, sn = np.cos(inner), np.sin(inner)
    wide = np.block([[c, -sn], [sn, c]])
    return (
        first.astype(np.float32),
        np.cos(turn).astype(np.float32),
        np.sin(turn).astype(np.float32),
        wide.astype(np.float32),
    )


def body(query_input, key_input, value_input, implicit_filter, explicit_taps, skip_gain, out_grad):
    rows, chans = query_input.shape
    n = lax.axis_size("ctx")
    me = lax.axis_index("ctx")
    mine = chans // n
    scale = 1.0 / math.sqrt(n * rows)
    first, cos_turn, sin_turn, wide = tables(n, rows)
    hi = lax.Precision.HIGHEST
    q = query_input.astype(jnp.float32)
    k = key_input.astype(jnp.float32)
    v = value_input.astype(jnp.float32)
    og = out_grad.astype(jnp.float32)
    prod = k * v
    mix = og * q
    extra = explicit_taps.at[0].add(skip_gain)
    filt = implicit_filter + jnp.where(me == 0, extra, 0.0)
    fields = jnp.stack([prod, filt, mix])
    sent = jnp.transpose(fields, (2, 0, 1)).reshape(n, mine, 3, rows)
    got = lax.all_to_all(sent, "ctx", 0, 0, tiled=True)
    a = jnp.einsum("ks,scft->kcft", first, got, precision=hi)
    ar, ai = a[:n], a[n:]
    ct, st = cos_turn[:, None, None, :], sin_turn[:, None, None, :]
    b = jnp.concatenate([ar * ct + ai * st, ai * ct - ar * st], axis=-1)
    x = jnp.einsum("kcft,tu->kcfu", b, wide, precision=hi)
    xr, xi = x[..., :rows], x[..., rows:]
    pr, pi, hr, hm, gr, gi = xr[:, :, 0], xi[:, :, 0], xr[:, :, 1], xi[:, :, 1], xr[:, :, 2], xi[:, :, 2]
    yr = jnp.stack([hr * pr - hm * pi, hr * gr + hm * gi, pr * gr + pi * gi], axis=2)
    yi = jnp.stack([hr * pi + hm * pr, hr * gi - hm * gr, pr * gi - pi * gr], axis=2)
    y = jnp.concatenate([yr, -yi], axis=-1)
    z = jnp.einsum("kcft,tu->kcfu", y, wide, precision=hi)
    zr, zi = z[..., :rows], -z[..., rows:]
    d = jnp.concatenate([zr * ct - zi * st, zi * ct + zr * st], axis=0)
    out = jnp.einsum("ks,kcft->scft", first * (1.0 / (n * rows)), d, precision=hi)
    lead = jnp.broadcast_to(out[:1, :, 2:], (n, mine, 1, rows))
    back = lax.all_to_all(jnp.concatenate([out, lead], axis=2), "ctx", 0, 0, tiled=True)
    res = jnp.transpose(back.reshape(chans, 4, rows), (1, 2, 0))
    mixer, pgrad, fgrad, tgrad = res[0], res[1], res[2] * scale, res[3] * scale
    return q * mixer, og * mixer, pgrad * v, pgrad * k, fgrad, tgrad, tgrad[0]


def solution(mesh):
    wide = P("ctx", "ch")
    return jax.shard_map(
        body,
        mesh=mesh,
        in_specs=(wide, wide, wide, wide, P(None, "ch"), P("ch"), wide),
        out_specs=(wide, wide, wide, wide, wide, P(None, "ch"), P("ch")),
        check_vma=False,
    )
```

time: 884 us -> 78.3 us (0.09)
  the two profiles are of different devices: /device:TPU:1 before, /device:TPU:2 now
where the time goes in v1:
time: 78.3 us; the launch traced here: 77.7 us
  blocking collectives  63.1 us (81%)
  local copies, waits for them, and re-layouts  11.5 us (15%)
  matrix products  1.82 us (2%)
  between operations  0.9 us (1%)
    all_to_all x1, blocking collectives, body(): got = lax.all_to_all(sent, 'ctx', 0, 0, tiled=True)  36.8 us
    all_to_all x1, blocking collectives, body(): lax.all_to_all(jnp.concatenate([out, lead], axis=2), 'ctx', 0, 0, tiled=T...  26.4 us
    unnamed x34, local copies, waits for them, and re-layouts  10.1 us

profile of v1, /device:TPU:2, one launch (start us, length us, event | category | flops | bytes accessed | tf_op | source)
XLA Modules:
  0.0 77.7 jit_solution(15539126327769258269)
XLA Ops:
  0.6 0.0 copy-start.7
  0.6 0.9 %copy.68 = bf16[128,128]{0,1:T(8,128)(2,1)S(1)} copy(bf16[128,128]{1,0:T(8,128)(2,1)} %param.16) | data formatting | bytes 65536 | tf_op args[1]
  1.5 0.0 copy-done.7
  1.5 0.0 copy-start.8
  1.5 0.0 copy-start.9
  1.6 0.1 copy.69
  1.7 0.6 copy-done.8
  2.3 0.0 copy-start.3
  2.3 0.1 copy.67
  2.4 0.0 copy-done.9
  2.4 0.1 copy.73
  2.5 0.6 copy-done.3
  3.1 0.0 copy-start.4
  3.1 0.1 copy.72
  3.2 0.7 copy-done.4
  4.0 0.0 copy-start.10
  4.0 0.1 copy.70
  4.1 0.6 copy-done.10
  4.6 0.1 copy.71
  4.8 0.3 scatter-add.4
  5.1 0.1 copy.74
  5.2 0.0 copy-start.6
  5.2 36.8 %all_to_all.10 = f32[64,2,3,128]{3,1,2,0:T(2,128)S(1)} all-to-all(f32[64,2,3,128]{3,1,2,0:T(2,128)S(1)} %copy.74), channel_id=1, replica_groups=mesh['ctx'=64,'ch'=8] {'ctx'}, dimensions={0} | all-to-all | bytes 393216 | tf_op jit(solution)/shard_map/all_to_all | solution.py:46
  41.9 0.0 copy-done.6
  41.9 0.0 copy-start.1
  41.9 0.0 copy-start.2
  41.9 0.5 fusion.16
  42.5 0.2 copy-done.1
  42.7 0.0 copy-done.2
  42.7 0.0 copy-start
  42.8 0.9 %copy-done = f32[256,256,1,1]{1,0,3,2:T(8,128)S(1)} copy-done((f32[256,256,1,1]{1,0,3,2:T(8,128)S(1)}, f32[256,256,1,1]{1,0,3,2:T(8,128)}, u32[]{:S(2)}) %copy-start) | copy-done | bytes 262168
  43.7 0.5 fusion
  44.2 0.5 fusion.4
  44.7 0.0 copy-start.5
  44.7 0.1 multiply_subtract_fusion
  44.8 0.7 copy-done.5
  45.5 0.3 fusion.12
  45.9 0.2 copy.76
  46.1 26.4 %all_to_all.11 = f32[64,2,4,128]{3,2,1,0:T(4,128)S(1)} all-to-all(f32[64,2,4,128]{3,2,1,0:T(4,128)S(1)} %copy.76), channel_id=1, replica_groups=mesh['ctx'=64,'ch'=8] {'ctx'}, dimensions={0} | all-to-all | bytes 524288 | tf_op jit(solution)/shard_map/all_to_all | solution.py:62
  72.5 0.1 copy.77
  72.7 0.7 copy.78
  73.4 0.7 copy.79
  74.1 0.7 copy.80
  74.9 0.7 copy.81
  75.6 0.7 copy.82
  76.3 0.7 copy.83
  77.0 0.6 slice_reduce_fusion
  (13 shorter events, 0.2 us)
Async XLA Ops:
  0.6 0.9 %copy-start.7 = (bf16[128,128]{1,0:T(8,128)(2,1)S(1)}, bf16[128,128]{1,0:T(8,128)(2,1)}, u32[]{:S(2)}) copy-start(bf16[128,128]{1,0:T(8,128)(2,1)} %param.17) | copy-start | bytes 98308
  1.5 0.8 copy-start.8
  1.5 0.9 %copy-start.9 = (bf16[128,128]{1,0:T(8,128)(2,1)S(1)}, bf16[128,128]{1,0:T(8,128)(2,1)}, u32[]{:S(2)}) copy-start(bf16[128,128]{1,0:T(8,128)(2,1)} %param.21) | copy-start | bytes 98308
  2.3 0.8 %copy-start.3 = (f32[128,128]{1,0:T(8,128)S(1)}, f32[128,128]{1,0:T(8,128)}, u32[]{:S(2)}) copy-start(f32[128,128]{1,0:T(8,128)} %param.18) | copy-start | bytes 196612
  3.1 0.8 %copy-start.4 = (f32[128,128]{1,0:T(8,128)S(1)}, f32[128,128]{1,0:T(8,128)}, u32[]{:S(2)}) copy-start(f32[128,128]{1,0:T(8,128)} %param.19) | copy-start | bytes 196612
  4.0 0.7 copy-start.10
  5.2 36.8 %copy-start.6 = (f32[128,64,1,1]{0,1,3,2:T(8,128)S(1)}, f32[128,64,1,1]{0,1,3,2:T(8,128)}, u32[]{:S(2)}) copy-start(f32[128,64,1,1]{0,1,3,2:T(8,128)} %constant.57) | copy-start | bytes 98308
  41.9 0.8 copy-start.1
  41.9 0.8 copy-start.2
  42.7 0.9 %copy-start = (f32[256,256,1,1]{1,0,3,2:T(8,128)S(1)}, f32[256,256,1,1]{1,0,3,2:T(8,128)}, u32[]{:S(2)}) copy-start(f32[256,256,1,1]{1,0,3,2:T(8,128)} %constant.58) | copy-start | bytes 786436
  44.7 0.8 copy-start.5

commit v2 on v1

v2 whole, which is shorter than its diff:
```python
import functools
import math

import jax
import jax.numpy as jnp
import numpy as np
from jax import lax
from jax.experimental import pallas as pl
from jax.experimental.pallas import tpu as pltpu
from jax.sharding import PartitionSpec as P

HIGHEST = lax.Precision.HIGHEST


def tables(blocks, rows):
    s = np.arange(blocks)
    t = np.arange(rows)
    k1 = s + 0.25
    outer = 2 * np.pi * np.outer(k1, s) / blocks
    first = np.concatenate([np.cos(outer), -np.sin(outer)], axis=0)
    last = first.T / (blocks * rows)
    turn = 2 * np.pi * np.outer(k1, t) / (blocks * rows)
    turn = np.concatenate([np.cos(turn), np.sin(turn)], axis=1)
    inner = 2 * np.pi * (np.outer(t, t) % rows) / rows
    c, sn = np.cos(inner), np.sin(inner)
    wide = np.block([[c, -sn], [sn, c]])
    return tuple(jnp.asarray(a.astype(np.float32)) for a in (first, last, turn, wide))


def dot(a, b):
    return lax.dot_general(
        a, b, (((1,), (0,)), ((), ())), precision=HIGHEST, preferred_element_type=jnp.float32
    )


def peer_at(step, me, ny, nz):
    i = step // ny
    dy = step % ny
    mag = nz // 2 - (i + 1) // 2
    odd = i % 2
    dz = odd * mag + (1 - odd) * (nz - mag)
    z = (me % nz + dz) % nz
    y = (me // nz + dy) % ny
    return y * nz + z


def mix_kernel(
    n, nz,
    q_in, k_in, v_in, f_in, taps_in, skip_in, og_in, first_in, last_in, turn_in, wide_in,
    out,
    q, k, v, f, taps, skip, og, first, last, turn, wide,
    sent, got, back,
    load_sems, table_sem, own_sem, send_sem, recv_sem, send2_sem, recv2_sem,
):
    ny = n // nz
    me = lax.axis_index("ctx")
    ch = lax.axis_index("ch")
    loads = [
        pltpu.make_async_copy(src, dst, load_sems.at[i])
        for i, (src, dst) in enumerate(
            ((q_in, q), (k_in, k), (v_in, v), (f_in, f), (taps_in, taps), (skip_in, skip), (og_in, og))
        )
    ]
    fetch = [
        pltpu.make_async_copy(src, dst, table_sem.at[i])
        for i, (src, dst) in enumerate(((first_in, first), (last_in, last), (turn_in, turn), (wide_in, wide)))
    ]
    for copy in loads + fetch:
        copy.start()

    barrier = pltpu.get_barrier_semaphore()

    def greet(step, carry):
        pl.semaphore_signal(
            barrier, inc=1, device_id=(peer_at(step, me, ny, nz), ch), device_id_type=pl.DeviceIdType.MESH
        )
        return carry

    steps = n - ny
    lax.fori_loop(0, steps, greet, 0)
    lax.fori_loop(steps + 1, n, greet, 0)

    for copy in loads:
        copy.wait()
    prod = k[...].astype(jnp.float32) * v[...].astype(jnp.float32)
    mix = og[...].astype(jnp.float32) * q[...].astype(jnp.float32)
    rows = prod.shape[0]
    at_zero = lax.broadcasted_iota(jnp.int32, prod.shape, 0) == 0
    extra = taps[...] + jnp.where(at_zero, skip[...], 0.0)
    filt = f[...] + jnp.where(me == 0, extra, 0.0)
    for j, field in enumerate((prod, filt, mix)):
        turned = field.T
        for c in range(2):
            sent[pl.ds(2 * j + c, n, stride=6), :] = turned[c * n : (c + 1) * n]

    pl.semaphore_wait(barrier, n - 1)

    own = pltpu.make_async_copy(sent.at[pl.ds(6 * me, 6)], got.at[pl.ds(6 * me, 6)], own_sem)
    own.start()

    def push(src, dst, size, ssem, rsem):
        def go(step, carry):
            peer = peer_at(step, me, ny, nz)
            pltpu.make_async_remote_copy(
                src_ref=src.at[pl.ds(size * peer, size)],
                dst_ref=dst.at[pl.ds(size * me, size)],
                send_sem=ssem,
                recv_sem=rsem,
                device_id=(peer, ch),
                device_id_type=pl.DeviceIdType.MESH,
            ).start()
            return carry

        lax.fori_loop(0, steps, go, 0)
        lax.fori_loop(steps + 1, n, go, 0)

    def all_of(src, dst, size, ssem, rsem):
        return pltpu.make_async_remote_copy(
            src_ref=src.at[pl.ds(0, size * (n - 1))],
            dst_ref=dst.at[pl.ds(0, size * (n - 1))],
            send_sem=ssem,
            recv_sem=rsem,
            device_id=((me + 1) % n, ch),
            device_id_type=pl.DeviceIdType.MESH,
        )

    push(sent, got, 6, send_sem, recv_sem)
    for copy in fetch:
        copy.wait()
    own.wait()
    all_of(sent, got, 6, send_sem, recv_sem).wait_recv()

    x = jnp.concatenate([got[pl.ds(j, n, stride=6), :] for j in range(6)], axis=1)
    a = dot(first[...], x)
    ct, st = turn[:, :rows], turn[:, rows:]
    parts = []
    for j in range(6):
        ar = a[:n, j * rows : (j + 1) * rows]
        ai = a[n:, j * rows : (j + 1) * rows]
        parts.append(jnp.concatenate([ar * ct + ai * st, ai * ct - ar * st], axis=1))
    w = wide[...]
    x = dot(jnp.concatenate(parts, axis=0), w)

    def spectrum(j):
        block = x[j * n : (j + 1) * n]
        return block[:, :rows], block[:, rows:]

    parts = [None] * 6
    for c in range(2):
        (pr, pi), (hr, hi), (gr, gi) = spectrum(c), spectrum(2 + c), spectrum(4 + c)
        parts[c] = jnp.concatenate([pr * gr + pi * gi, pi * gr - pr * gi], axis=1)
        parts[2 + c] = jnp.concatenate([hr * pr - hi * pi, -hr * pi - hi * pr], axis=1)
        parts[4 + c] = jnp.concatenate([hr * gr + hi * gi, hi * gr - hr * gi], axis=1)
    z = dot(jnp.concatenate(parts, axis=0), w)
    res, ims = [], []
    for j in range(6):
        zr = z[j * n : (j + 1) * n, :rows]
        zi = z[j * n : (j + 1) * n, rows:]
        res.append(zr * ct + zi * st)
        ims.append(zr * st - zi * ct)
    d = jnp.concatenate([jnp.concatenate(res, axis=1), jnp.concatenate(ims, axis=1)], axis=0)
    y = dot(last[...], d)
    for j in range(6):
        piece = y[:, j * rows : (j + 1) * rows]
        back[pl.ds(j, n, stride=8), :] = piece
        if j < 2:
            back[pl.ds(6 + j, n, stride=8), :] = jnp.broadcast_to(piece[:1], (n, rows))

    own = pltpu.make_async_copy(back.at[pl.ds(8 * me, 8)], out.at[pl.ds(8 * me, 8)], own_sem)
    own.start()
    push(back, out, 8, send2_sem, recv2_sem)
    own.wait()
    all_of(back, out, 8, send2_sem, recv2_sem).wait_recv()
    all_of(sent, got, 6, send_sem, recv_sem).wait_send()
    all_of(back, out, 8, send2_sem, recv2_sem).wait_send()


def close_kernel(n, scale, got, q, k, v, og, *refs):
    outs, bufs, sems = refs[:7], refs[7:14], refs[14]

    def whole(j):
        return jnp.concatenate([got[pl.ds(2 * j + c, n, stride=8), :] for c in range(2)], axis=0).T

    copies = [pltpu.make_async_copy(b, o, sems.at[i]) for i, (b, o) in enumerate(zip(bufs, outs))]
    lead = whole(3) * scale
    bufs[4][...] = whole(0) * scale
    bufs[5][...] = lead
    bufs[6][...] = lead[:1]
    mixer = whole(1)
    bufs[0][...] = q[...].astype(jnp.float32) * mixer
    bufs[1][...] = og[...].astype(jnp.float32) * mixer
    for i in (4, 5, 6, 0, 1):
        copies[i].start()
    pgrad = whole(2)
    bufs[2][...] = pgrad * v[...].astype(jnp.float32)
    bufs[3][...] = pgrad * k[...].astype(jnp.float32)
    for i in (2, 3):
        copies[i].start()
    for copy in copies:
        copy.wait()


def body(nz, query_input, key_input, value_input, implicit_filter, explicit_taps, skip_gain, out_grad):
    rows, chans = query_input.shape
    n = lax.axis_size("ctx")
    scale = 1.0 / math.sqrt(n * rows)
    first, last, turn, wide = tables(n, rows)
    f32, bf16 = jnp.float32, jnp.bfloat16
    vmem = pl.BlockSpec(memory_space=pltpu.VMEM)
    anywhere = pl.BlockSpec(memory_space=pl.ANY)
    tile = pltpu.VMEM((rows, chans), bf16)
    full = pltpu.VMEM((rows, chans), f32)
    got = pl.pallas_call(
        functools.partial(mix_kernel, n, nz),
        name="mix",
        out_shape=jax.ShapeDtypeStruct((8 * n, rows), f32),
        in_specs=[anywhere] * 11,
        out_specs=vmem,
        scratch_shapes=[
            tile, tile, tile, full, full, pltpu.VMEM((1, chans), f32), tile,
            *[pltpu.VMEM(t.shape, f32) for t in (first, last, turn, wide)],
            pltpu.VMEM((6 * n, rows), f32),
            pltpu.VMEM((6 * n, rows), f32),
            pltpu.VMEM((8 * n, rows), f32),
            pltpu.SemaphoreType.DMA((7,)),
            pltpu.SemaphoreType.DMA((4,)),
            *[pltpu.SemaphoreType.DMA] * 5,
        ],
        compiler_params=pltpu.CompilerParams(collective_id=0, has_side_effects=True),
    )(
        query_input, key_input, value_input, implicit_filter, explicit_taps,
        skip_gain.reshape(1, chans), out_grad, first, last, turn, wide,
    )
    wide_out = jax.ShapeDtypeStruct((rows, chans), f32)
    outs = pl.pallas_call(
        functools.partial(close_kernel, n, scale),
        name="close",
        out_shape=[wide_out] * 6 + [jax.ShapeDtypeStruct((1, chans), f32)],
        in_specs=[vmem] * 5,
        out_specs=[anywhere] * 7,
        scratch_shapes=[full] * 6 + [pltpu.VMEM((1, chans), f32), pltpu.SemaphoreType.DMA((7,))],
    )(got, query_input, key_input, value_input, out_grad)
    return (*outs[:6], outs[6].reshape(chans))


def solution(mesh):
    wide = P("ctx", "ch")
    nz = math.gcd(16, mesh.shape["ctx"])
    return jax.shard_map(
        functools.partial(body, nz),
        mesh=mesh,
        in_specs=(wide, wide, wide, wide, P(None, "ch"), P("ch"), wide),
        out_specs=(wide, wide, wide, wide, wide, P(None, "ch"), P("ch")),
        check_vma=False,
    )
```

time: 78.3 us -> 48.7 us (0.62)
  the two profiles are of different devices: /device:TPU:2 before, /device:TPU:1 now
where the time goes in v2:
time: 48.7 us; the launch traced here: 48.6 us
  Pallas kernels  47.9 us (98%)
  between operations  0.64 us (1%)
    pallas_call x1, Pallas kernels, body(): pl.pallas_call(functools.partial(mix_kernel, n, nz), name='mix', out_shap...  46 us
    pallas_call x1, Pallas kernels, body(): pl.pallas_call(functools.partial(close_kernel, n, scale), name='close', o...  1.91 us

profile of v2, /device:TPU:1, one launch (start us, length us, event | category | flops | bytes accessed | tf_op | source)
XLA Modules:
  0.0 48.6 jit_solution(4620199019012056854)
XLA Ops:
  0.6 46.0 %mix.1.got = f32[512,128]{1,0:T(8,128)} custom-call(bf16[128,128]{1,0:T(8,128)(2,1)} %q.1, bf16[128,128]{1,0:T(8,128)(2,1)} %k.1, bf16[128,128]{1,0:T(8,128)(2,1)} %v.1, f32[128,128]{1,0:T(8,128)} %f_in.1, f32[128,128]{1,0:T(8,128)} %taps_in.1, f32[1,128]{1,0:T(1,128)} %bitcast.2, bf16[128,128]{1,0:T(8,128)(2,1)} %og.1, f32[128,64]{1,0:T(8,128)} %constant.8.clone.first_in, ...), custom_call_target="tpu_custom_call" | custom-call | tf_op jit(solution)/shard_map/mix/pallas_call | solution.py:213
  46.7 1.9 %close.1 = (f32[128,128]{1,0:T(8,128)}, f32[128,128]{1,0:T(8,128)}, f32[128,128]{1,0:T(8,128)}, f32[128,128]{1,0:T(8,128)}, f32[128,128]{1,0:T(8,128)}, /*index=5*/f32[128,128]{1,0:T(8,128)}, f32[1,128]{1,0:T(1,128)}) custom-call(f32[512,128]{1,0:T(8,128)} %mix.1.got, bf16[128,128]{1,0:T(8,128)(2,1)} %q.1, bf16[128,128]{1,0:T(8,128)(2,1)} %k.1, ...), custom_call_target="tpu_custom_call" | custom-call | tf_op jit(solution)/shard_map/close/pallas_call | solution.py:235

commit v3 on v1

v3 whole, which is shorter than its diff:
```python
import functools
import math

import jax
import jax.numpy as jnp
import numpy as np
from jax import lax
from jax.experimental import pallas as pl
from jax.experimental.pallas import tpu as pltpu
from jax.sharding import PartitionSpec as P

F32, BF16 = jnp.float32, jnp.bfloat16
MESH = pl.DeviceIdType.MESH


def halves(table):
    high = table.astype(np.float32).astype(BF16)
    low = (table - high.astype(np.float64)).astype(np.float32).astype(BF16)
    return high, low


def tables(blocks, rows):
    s = np.arange(blocks)
    t = np.arange(rows)
    k1 = s + 0.25
    outer = 2 * np.pi * np.outer(k1, s) / blocks
    first = np.concatenate([np.cos(outer), -np.sin(outer)], axis=0)
    last = first.T / (blocks * rows)
    turn = 2 * np.pi * np.outer(k1, t) / (blocks * rows)
    turn = np.concatenate([np.cos(turn), np.sin(turn)], axis=1).astype(np.float32)
    inner = 2 * np.pi * (np.outer(t, t) % rows) / rows
    c, sn = np.cos(inner), np.sin(inner)
    wide = np.block([[c, -sn], [sn, c]])
    fh, fl = halves(first)
    lh, ll = halves(last)
    first3 = np.concatenate([fh, fh, fl], axis=1)
    last3 = np.concatenate([lh, lh, ll], axis=1)
    return tuple(jnp.asarray(a) for a in (first3, last3, turn, *halves(wide)))


def mm(a, b):
    return lax.dot_general(a, b, (((1,), (0,)), ((), ())), preferred_element_type=F32)


def split(x):
    high = x.astype(BF16)
    return high, (x - high.astype(F32)).astype(BF16)


def left(table3, x):
    high, low = split(x)
    return mm(table3, jnp.concatenate([high, low, high], axis=0))


def right(x, w_high, w_low):
    high, low = split(x)
    both = mm(jnp.concatenate([high, low], axis=0), w_high)
    return both[: x.shape[0]] + both[x.shape[0] :] + mm(high, w_low)


def far_first(i, nz):
    mag = nz // 2 - (i + 1) // 2
    odd = i % 2
    return odd * mag + (1 - odd) * (nz - mag)


def mix_kernel(
    n, nz,
    q_in, k_in, v_in, f_in, taps_in, skip_in, og_in, first_in, last_in, turn_in, wide_in, wlow_in,
    lag, main, lead, q, k, v, og,
    f, taps, skip, first, last, turn, wide, wlow,
    sent, got, lag_out, main_out, row,
    load_sems, table_sems, own_sems, send_sems, recv_sems,
):
    ny = n // nz
    me = lax.axis_index("ctx")
    ch = lax.axis_index("ch")
    my_z = me % nz
    my_y = me // nz
    loads = [
        pltpu.make_async_copy(src, dst, load_sems.at[i])
        for i, (src, dst) in enumerate(
            ((q_in, q), (k_in, k), (v_in, v), (f_in, f), (taps_in, taps), (skip_in, skip), (og_in, og))
        )
    ]
    fetch = [
        pltpu.make_async_copy(src, dst, table_sems.at[i])
        for i, (src, dst) in enumerate(
            ((first_in, first), (last_in, last), (turn_in, turn), (wide_in, wide), (wlow_in, wlow))
        )
    ]
    for copy in loads + fetch:
        copy.start()

    def peer_at(step):
        z = (my_z + far_first(step // ny, nz)) % nz
        y = (my_y + step % ny) % ny
        return y * nz + z

    def each_peer(visit):
        def go(step, carry):
            visit(peer_at(step))
            return carry

        away = n - ny
        lax.fori_loop(0, away, go, 0)
        lax.fori_loop(away + 1, n, go, 0)

    barrier = pltpu.get_barrier_semaphore()
    each_peer(lambda peer: pl.semaphore_signal(barrier, inc=1, device_id=(peer, ch), device_id_type=MESH))

    for copy in loads:
        copy.wait()
    prod = k[...].astype(F32) * v[...].astype(F32)
    mix = og[...].astype(F32) * q[...].astype(F32)
    rows = prod.shape[0]
    at_zero = lax.broadcasted_iota(jnp.int32, prod.shape, 0) == 0
    extra = taps[...] + jnp.where(at_zero, skip[...], 0.0)
    filt = f[...] + jnp.where(me == 0, extra, 0.0)
    for j, field in enumerate((prod, filt, mix)):
        turned = field.T
        for c in range(2):
            sent[pl.ds(2 * j + c, n, stride=6), :] = turned[c * n : (c + 1) * n]

    pl.semaphore_wait(barrier, n - 1)

    def remote(src, dst, i, peer):
        return pltpu.make_async_remote_copy(
            src_ref=src,
            dst_ref=dst,
            send_sem=send_sems.at[i],
            recv_sem=recv_sems.at[i],
            device_id=(peer, ch),
            device_id_type=MESH,
        )

    def push(src, dst, size, i):
        own = pltpu.make_async_copy(
            src.at[pl.ds(size * me, size)], dst.at[pl.ds(size * me, size)], own_sems.at[i]
        )
        own.start()
        each_peer(
            lambda peer: remote(
                src.at[pl.ds(size * peer, size)], dst.at[pl.ds(size * me, size)], i, peer
            ).start()
        )
        return own

    def total(src, dst, amount, i):
        return remote(src.at[pl.ds(0, amount)], dst.at[pl.ds(0, amount)], i, (me + 1) % n)

    own = push(sent, got, 6, 0)
    for copy in fetch:
        copy.wait()
    own.wait()
    forward = total(sent, got, 6 * (n - 1), 0)
    forward.wait_recv()

    x = jnp.concatenate([got[pl.ds(j, n, stride=6), :] for j in range(6)], axis=1)
    a = left(first[...], x)
    ct, st = turn[:, :rows], turn[:, rows:]
    parts = []
    for j in range(6):
        ar = a[:n, j * rows : (j + 1) * rows]
        ai = a[n:, j * rows : (j + 1) * rows]
        parts.append(jnp.concatenate([ar * ct + ai * st, ai * ct - ar * st], axis=1))
    x = right(jnp.concatenate(parts, axis=0), wide[...], wlow[...])

    def spectrum(j):
        block = x[j * n : (j + 1) * n]
        return block[:, :rows], block[:, rows:]

    def to_time(conjugates):
        z = right(jnp.concatenate(conjugates, axis=0), wide[...], wlow[...])
        res, ims = [], []
        for j in range(len(conjugates)):
            zr = z[j * n : (j + 1) * n, :rows]
            zi = z[j * n : (j + 1) * n, rows:]
            res.append(zr * ct + zi * st)
            ims.append(zr * st - zi * ct)
        d = jnp.concatenate([jnp.concatenate(res, axis=1), jnp.concatenate(ims, axis=1)], axis=0)
        y = left(last[...], d)
        return [y[:, j * rows : (j + 1) * rows] for j in range(len(conjugates))]

    def conj_of(ar, ai, br, bi):
        return jnp.concatenate([ar * br + ai * bi, ai * br - ar * bi], axis=1)

    spectra = [(spectrum(c), spectrum(2 + c), spectrum(4 + c)) for c in range(2)]
    for c, piece in enumerate(to_time([conj_of(*p, *g) for p, _, g in spectra])):
        lag_out[pl.ds(c, n, stride=2), :] = piece
        row[pl.ds(c, 1), :] = piece[:1]

    mine = pl.ds(pl.multiple_of(2 * my_z, 2), 2)
    near = lead.at[pl.ds(pl.multiple_of(2 * nz * my_y, 2 * nz), 2 * nz)]
    lead_own = pltpu.make_async_copy(row, near.at[mine], own_sems.at[3])
    lead_own.start()

    def along_z(i, carry):
        peer = my_y * nz + (my_z + far_first(i, nz)) % nz
        remote(row, near.at[mine], 3, peer).start()
        return carry

    lax.fori_loop(0, nz - 1, along_z, 0)
    lag_own = push(lag_out, lag, 2, 1)

    out = [jnp.concatenate([hr * pr - hi * pi, -(hr * pi + hi * pr)], axis=1) for (pr, pi), (hr, hi), _ in spectra]
    back = [conj_of(*h, *g) for _, h, g in spectra]
    for j, piece in enumerate(to_time(out + back)):
        main_out[pl.ds(j, n, stride=4), :] = piece
    main_own = push(main_out, main, 4, 2)

    lead_own.wait()
    by_z = remote(near.at[pl.ds(0, 2 * (nz - 1))], near.at[pl.ds(0, 2 * (nz - 1))], 3, (me + 1) % n)
    by_z.wait_recv()

    def along_y(step, carry):
        peer = (my_y + step) % ny * nz + my_z
        remote(near, near, 4, peer).start()
        return carry

    lax.fori_loop(1, ny, along_y, 0)

    lag_own.wait()
    main_own.wait()
    by_y = total(lead, lead, 2 * nz * (ny - 1), 4)
    lags = total(lag_out, lag, 2 * (n - 1), 1)
    mains = total(main_out, main, 4 * (n - 1), 2)
    lags.wait_recv()
    mains.wait_recv()
    by_y.wait_recv()
    for copy in (forward, lags, mains, by_z, by_y):
        copy.wait_send()


def close_kernel(n, scale, lag, main, lead, q, k, v, og, *refs):
    outs, bufs, sems = refs[:7], refs[7:14], refs[14]

    def whole(ref, j, step):
        return jnp.concatenate([ref[pl.ds(j + c, n, stride=step), :] for c in range(2)], axis=0).T

    copies = [pltpu.make_async_copy(b, o, sems.at[i]) for i, (b, o) in enumerate(zip(bufs, outs))]

    def put(i, value):
        bufs[i][...] = value
        copies[i].start()

    put(4, whole(lag, 0, 2) * scale)
    first_lags = whole(lead, 0, 2) * scale
    put(5, first_lags)
    put(6, first_lags[:1])
    mixer = whole(main, 0, 4)
    put(0, q[...].astype(F32) * mixer)
    put(1, og[...].astype(F32) * mixer)
    pgrad = whole(main, 2, 4)
    put(2, pgrad * v[...].astype(F32))
    put(3, pgrad * k[...].astype(F32))
    for copy in copies:
        copy.wait()


def body(nz, query_input, key_input, value_input, implicit_filter, explicit_taps, skip_gain, out_grad):
    rows, chans = query_input.shape
    n = lax.axis_size("ctx")
    scale = 1.0 / math.sqrt(n * rows)
    consts = tables(n, rows)
    vmem = pl.BlockSpec(memory_space=pltpu.VMEM)
    anywhere = pl.BlockSpec(memory_space=pl.ANY)
    tile = pltpu.VMEM((rows, chans), BF16)
    full = pltpu.VMEM((rows, chans), F32)
    one = pltpu.VMEM((1, chans), F32)

    def stack(count):
        return pltpu.VMEM((count, rows), F32)

    held = pl.pallas_call(
        functools.partial(mix_kernel, n, nz),
        name="mix",
        out_shape=[stack(2 * n), stack(4 * n), stack(2 * n), tile, tile, tile, tile],
        in_specs=[anywhere] * 12,
        out_specs=[vmem] * 7,
        scratch_shapes=[
            full, full, one,
            *[pltpu.VMEM(t.shape, t.dtype) for t in consts],
            stack(6 * n), stack(6 * n), stack(2 * n), stack(4 * n), stack(2),
            pltpu.SemaphoreType.DMA((7,)),
            pltpu.SemaphoreType.DMA((len(consts),)),
            pltpu.SemaphoreType.DMA((4,)),
            pltpu.SemaphoreType.DMA((5,)),
            pltpu.SemaphoreType.DMA((5,)),
        ],
        compiler_params=pltpu.CompilerParams(collective_id=0, has_side_effects=True),
    )(
        query_input, key_input, value_input, implicit_filter, explicit_taps,
        skip_gain.reshape(1, chans), out_grad, *consts,
    )
    held = [pltpu.with_memory_space_constraint(x, pltpu.VMEM) for x in held]
    wide_out = jax.ShapeDtypeStruct((rows, chans), F32)
    outs = pl.pallas_call(
        functools.partial(close_kernel, n, scale),
        name="close",
        out_shape=[wide_out] * 6 + [jax.ShapeDtypeStruct((1, chans), F32)],
        in_specs=[vmem] * 7,
        out_specs=[anywhere] * 7,
        scratch_shapes=[full] * 6 + [one, pltpu.SemaphoreType.DMA((7,))],
    )(*held)
    return (*outs[:6], outs[6].reshape(chans))


def solution(mesh):
    wide = P("ctx", "ch")
    nz = math.gcd(16, mesh.shape["ctx"])
    return jax.shard_map(
        functools.partial(body, nz),
        mesh=mesh,
        in_specs=(wide, wide, wide, wide, P(None, "ch"), P("ch"), wide),
        out_specs=(wide, wide, wide, wide, wide, P(None, "ch"), P("ch")),
        check_vma=False,
    )
```

time: 78.3 us -> 44.5 us (0.57)
  the two profiles are of different devices: /device:TPU:2 before, /device:TPU:1 now
where the time goes in v3:
time: 44.5 us; the launch traced here: 44.2 us
  Pallas kernels  43.6 us (98%)
  between operations  0.64 us (1%)
    pallas_call x1, Pallas kernels, body(): pl.pallas_call(functools.partial(mix_kernel, n, nz), name='mix', out_shap...  42.6 us
    pallas_call x1, Pallas kernels, body(): pl.pallas_call(functools.partial(close_kernel, n, scale), name='close', o...  0.91 us

profile of v3, /device:TPU:1, one launch (start us, length us, event | category | flops | bytes accessed | tf_op | source)
XLA Modules:
  0.0 44.2 jit_solution(2245472308547266540)
XLA Ops:
  0.6 42.6 %mix.1 = (f32[128,128]{1,0:T(8,128)S(1)}, f32[256,128]{1,0:T(8,128)S(1)}, f32[128,128]{1,0:T(8,128)S(1)}, bf16[128,128]{1,0:T(8,128)(2,1)S(1)}, bf16[128,128]{1,...) custom-call(bf16[128,128]{1,0:T(8,128)(2,1)} %q_in.1, bf16[128,128]{1,0:T(8,128)(2,1)} %k_in.1, ...), custom_call_target="tpu_custom_call" | custom-call | tf_op jit(solution)/shard_map/mix/pallas_call | solution.py:275
  43.3 0.9 %close.1 = (f32[128,128]{1,0:T(8,128)}, f32[128,128]{1,0:T(8,128)}, f32[128,128]{1,0:T(8,128)}, f32[128,128]{1,0:T(8,128)}, f32[128,128]{1,0:T(8,128)}, /*index=5*/f32[128,128]{1,0:T(8,128)}, f32[1,128]{1,0:T(1,128)}) custom-call(f32[128,128]{1,0:T(8,128)S(1)} %get-tuple-element.21.lag, f32[256,128]{1,0:T(8,128)S(1)} %get-tuple-element.22.main, ...), custom_call_target="tpu_custom_call" | custom-call | tf_op jit(solution)/shard_map/close/pallas_call | solution.py:298
